TPU v7x, 32 devices: a whole 2x2x4 slice. The times are simulated.
32 devices in a mesh: grp: 2 (over x), band: 16 (over z, y, core).
Axes of the slice: x: 2, y: 2, z: 4, core: 2. Of those that a mesh axis runs over, the one named last changes fastest.
Arguments:
- samples: float32 [2, 192, 8192], P(None, None, ('grp', 'band')), parts along dimension 2, may hold values from -6 to 6
- prototype: float32 [16, 128], replicated, may hold values from -1.5 to 1.5
- dish_filter: float32 [2, 8, 192, 128], replicated, may hold values from -1.5 to 1.5
- beam_weights: float32 [16, 8, 2, 192, 192], P('band'), may hold values from -0.3125 to 0.3125
- dish_order: int32 [192], replicated, may hold values from 0 to 191, each once
Outputs:
- power: float32 [32, 8, 192, 8], P(('grp', 'band')), parts along dimension 0
There are 2 independent parts, one for each index of `grp`. A program takes and returns all parts, laid end to end along the dimension named above; an argument that names none is the same for every part. Nothing has to cross between parts.
Inputs may be any that keep to these rules, and one draw needn't show every extreme that they name: `dish_order`: each of the 192 dishes stands in exactly one panel slot.
All inputs are finite; a program needn't handle non-finite values.
Results may differ from a plain program's by a relative error of at most 0.0003.
Values sent between devices are 32-bit elements; how exact they have to be, the bound alone decides.
A program may use at most 64 MiB of HBM per device.

v0:
```python
import math

import jax
import jax.numpy as jnp
from jax import lax
from jax.sharding import PartitionSpec as P

INTEG = 4


def shifted(value, axis, steps):
    count = lax.axis_size(axis)
    leading, last = (max(0, -steps), min(count, count - steps))
    return lax.ppermute(value, axis, [(source, source + steps) for source in range(leading, last)])


def swapped(value, axis, bit):
    mask = 2**bit
    pairs = [(source, source ^ mask) for source in range(lax.axis_size(axis))]
    return lax.ppermute(value, axis, pairs)


def fourier_tables(length):
    counter = jnp.arange(length, dtype=jnp.int32)
    product = counter[:, None] * counter[None, :] % length
    angles = product.astype(jnp.float32) * (2.0 * math.pi / length)
    factor = 1.0 / math.sqrt(length)
    return (jnp.cos(angles) * factor, jnp.sin(angles) * factor)


def filter_frames(real_in, imag_in, tap_real, tap_imag, frame_count):
    tap_count = tap_real.shape[0]
    out_real = jnp.zeros(real_in.shape[:-1] + (frame_count,), real_in.dtype)
    out_imag = jnp.zeros(real_in.shape[:-1] + (frame_count,), real_in.dtype)
    for tap_index in range(tap_count):
        offset = tap_count - 1 - tap_index
        part_real = real_in[..., offset : offset + frame_count]
        part_imag = imag_in[..., offset : offset + frame_count]
        factor_real = tap_real[tap_index][..., None]
        factor_imag = tap_imag[tap_index][..., None]
        out_real = out_real + factor_real * part_real - factor_imag * part_imag
        out_imag = out_imag + factor_real * part_imag + factor_imag * part_real
    return (out_real, out_imag)


def detect(weights, field_real, field_imag):
    highest = lax.Precision.HIGHEST

    def contract(weight_part, field_part):
        return jnp.einsum("qds,dqf->qsf", weight_part, field_part, precision=highest)

    beam_real = contract(weights[:, 0], field_real) - contract(weights[:, 1], field_imag)
    beam_imag = contract(weights[:, 0], field_imag) + contract(weights[:, 1], field_real)
    energy = beam_real * beam_real + beam_imag * beam_imag
    shaped = energy.reshape(energy.shape[:-1] + (energy.shape[-1] // INTEG, INTEG))
    return jnp.mean(shaped, axis=-1)


def history(blocks, needed, frames_dev):
    pieces = [blocks]
    rounds = -(-needed // frames_dev)
    for step_count in range(1, rounds + 1):
        keeping = min(frames_dev, needed - (step_count - 1) * frames_dev)
        tail_part = blocks[:, :, frames_dev - keeping :, :]
        arrived_tail = shifted(tail_part, "band", step_count)
        pieces = [arrived_tail] + pieces
    return jnp.concatenate(pieces, axis=2)


def body(samples, prototype, dish_filter, beam_weights, dish_order):
    highest = lax.Precision.HIGHEST
    devices = lax.axis_size("band")
    position = lax.axis_index("band")
    pfb_count = prototype.shape[0]
    channels = prototype.shape[1]
    fir_count = dish_filter.shape[1]
    dishes = dish_filter.shape[2]
    band_chans = beam_weights.shape[1]
    bands = channels // band_chans
    owners = devices // bands
    panel_size = dishes // owners
    frames_dev = samples.shape[2] // channels
    band_id = position // owners
    owner_id = position % owners
    zero_index = jnp.zeros((), jnp.int32)
    ordered = jnp.take(samples, dish_order, axis=1)
    taps_ordered = jnp.take(dish_filter, dish_order, axis=2)
    blocks = ordered.reshape(2, dishes, frames_dev, channels)
    extended = history(blocks, pfb_count - 1, frames_dev)
    polyphase = jnp.zeros((2, dishes, frames_dev, channels), jnp.float32)
    for tap_index in range(pfb_count):
        offset = pfb_count - 1 - tap_index
        polyphase = (
            polyphase + prototype[tap_index] * extended[:, :, offset : offset + frames_dev, :]
        )
    cosine_table, sine_table = fourier_tables(channels)
    spec_real = jnp.dot(polyphase[0], cosine_table, precision=highest) + jnp.dot(
        polyphase[1], sine_table, precision=highest
    )
    spec_imag = jnp.dot(polyphase[1], cosine_table, precision=highest) - jnp.dot(
        polyphase[0], sine_table, precision=highest
    )
    spec_real = jnp.transpose(spec_real, (0, 2, 1))
    spec_imag = jnp.transpose(spec_imag, (0, 2, 1))
    stacked = jnp.stack([spec_real, spec_imag])
    pieces = stacked.reshape(2, owners, panel_size, bands, band_chans, frames_dev)
    pieces = jnp.transpose(pieces, (3, 1, 0, 2, 4, 5))
    pieces = pieces.reshape(devices, 2, panel_size, band_chans, frames_dev)
    arrived = lax.all_to_all(pieces, "band", split_axis=0, concat_axis=4, tiled=True)[0]
    total_frames = arrived.shape[3]
    dish_count = arrived.shape[1]
    if dish_count == dishes:
        dish_start = zero_index
    else:
        dish_start = owner_id * panel_size
    local_taps = lax.dynamic_slice(
        taps_ordered,
        (zero_index, zero_index, dish_start, band_id * band_chans),
        (2, fir_count, dish_count, band_chans),
    )
    padded = jnp.pad(arrived, ((0, 0), (0, 0), (0, 0), (fir_count - 1, 0)))
    filtered_real, filtered_imag = filter_frames(
        padded[0], padded[1], local_taps[0], local_taps[1], total_frames
    )
    arrived = jnp.stack([filtered_real, filtered_imag])
    collected = arrived[:, None]
    for bit_pos in range(owners.bit_length() - 1):
        partner = swapped(collected, "band", bit_pos)
        upper_half = owner_id // (1 << bit_pos) % 2 == 1
        collected = jnp.where(
            upper_half,
            jnp.concatenate([partner, collected], axis=1),
            jnp.concatenate([collected, partner], axis=1),
        )
    gathered = collected.reshape(2, dishes, band_chans, total_frames)
    power = detect(beam_weights[0], gathered[0], gathered[1])
    return power[None]


def solution(mesh):
    placed = (P(None, None, ("grp", "band")), P(), P(), P("band", None, None, None, None), P())
    return jax.shard_map(
        body,
        mesh=mesh,
        in_specs=placed,
        out_specs=P(("grp", "band"), None, None, None),
        check_vma=False,
    )
```

profile of v0, /device:TPU:0, one launch (start us, length us, event | category | flops | bytes accessed | tf_op | source)
XLA Modules:
  0.0 127.6 jit_solution(12866249529802294853)
XLA Ops:
  0.0 0.0 copy-start
  0.0 0.8 compare_and_fusion
  0.8 0.7 compare_select_fusion
  1.5 2.4 %gather_fusion.1 = f32[192,2,256]{2,0,1:T(8,128)S(1)} fusion(f32[2,192,256]{2,1,0:T(8,128)} %param.5, s32[1024]{0:T(1024)S(1)} %pad_clamp_fusion), kind=kCustom, calls=%fused_computation.1 | custom fusion | bytes 787200 | tf_op jit(solution)/shard_map/jit(_take)/gather | solution.py:86
  3.9 0.1 bitcast_select_fusion
  4.0 5.3 %collective-permute-start.6 = (f32[2,192,2,128]{3,1,2,0:T(8,128)S(1)}, f32[2,192,2,128]{3,1,2,0:T(8,128)S(1)}, u32[]{:S(2)}, u32[]{:S(2)}) collective-permute-start(f32[2,192,2,128]{3,1,2,0:T(8,128)S(1)} %bitcast_select_fusion), channel_id=1, source_target_pairs={{0,7},{1,8},{2,9},{3,10},{4,11},{5,12},{6,13},{7,14},{8,15},{16,23... | collective-permute-start | bytes 1179656 | tf_op jit(solution)/shard_map/ppermute | solution.py:14
  9.4 4.5 %collective-permute-start.5 = (f32[2,192,2,128]{3,1,2,0:T(8,128)S(1)}, f32[2,192,2,128]{3,1,2,0:T(8,128)S(1)}, u32[]{:S(2)}, u32[]{:S(2)}) collective-permute-start(f32[2,192,2,128]{3,1,2,0:T(8,128)S(1)} %bitcast_select_fusion), channel_id=1, source_target_pairs={{0,6},{1,7},{2,8},{3,9},{4,10},{5,11},{6,12},{7,13},{8,14},{9,15},... | collective-permute-start | bytes 1179656 | tf_op jit(solution)/shard_map/ppermute | solution.py:14
  13.9 1.9 %collective-permute-start.7 = (f32[2,192,1,128]{3,1,2,0:T(8,128)S(1)}, f32[2,192,1,128]{3,1,2,0:T(8,128)S(1)}, u32[]{:S(2)}, u32[]{:S(2)}) collective-permute-start(f32[2,192,1,128]{3,1,2,0:T(8,128)S(1)} %slice.303), channel_id=1, source_target_pairs={{0,8},{1,9},{2,10},{3,11},{4,12},{5,13},{6,14},{7,15},{16,24},{17,... | collective-permute-start | bytes 589832 | tf_op jit(solution)/shard_map/ppermute | solution.py:14
  15.8 1.3 %collective-permute-start.4 = (f32[2,192,2,128]{3,1,2,0:T(8,128)S(1)}, f32[2,192,2,128]{3,1,2,0:T(8,128)S(1)}, u32[]{:S(2)}, u32[]{:S(2)}) collective-permute-start(f32[2,192,2,128]{3,1,2,0:T(8,128)S(1)} %bitcast_select_fusion), channel_id=1, source_target_pairs={{0,5},{1,6},{2,7},{3,8},{4,9},{5,10},{6,11},{7,12},{8,13},{9,14},{... | collective-permute-start | bytes 1179656 | tf_op jit(solution)/shard_map/ppermute | solution.py:14
  17.2 1.6 %collective-permute-start.3 = (f32[2,192,2,128]{3,1,2,0:T(8,128)S(1)}, f32[2,192,2,128]{3,1,2,0:T(8,128)S(1)}, u32[]{:S(2)}, u32[]{:S(2)}) collective-permute-start(f32[2,192,2,128]{3,1,2,0:T(8,128)S(1)} %bitcast_select_fusion), channel_id=1, source_target_pairs={{0,4},{1,5},{2,6},{3,7},{4,8},{5,9},{6,10},{7,11},{8,12},{9,13},{1... | collective-permute-start | bytes 1179656 | tf_op jit(solution)/shard_map/ppermute | solution.py:14
  18.8 12.8 %collective-permute-done.7 = f32[2,192,1,128]{3,1,2,0:T(8,128)S(1)} collective-permute-done((f32[2,192,1,128]{3,1,2,0:T(8,128)S(1)}, f32[2,192,1,128]{3,1,2,0:T(8,128)S(1)}, u32[]{:S(2)}, u32[]{:S(2)}) %collective-permute-start.7) | collective-permute-done | bytes 196640 | tf_op jit(solution)/shard_map/ppermute | solution.py:14
  31.5 3.2 %collective-permute-start.2 = (f32[2,192,2,128]{3,1,2,0:T(8,128)S(1)}, f32[2,192,2,128]{3,1,2,0:T(8,128)S(1)}, u32[]{:S(2)}, u32[]{:S(2)}) collective-permute-start(f32[2,192,2,128]{3,1,2,0:T(8,128)S(1)} %bitcast_select_fusion), channel_id=1, source_target_pairs={{0,3},{1,4},{2,5},{3,6},{4,7},{5,8},{6,9},{7,10},{8,11},{9,12},{10... | collective-permute-start | bytes 1179656 | tf_op jit(solution)/shard_map/ppermute | solution.py:14
  34.8 0.0 collective-permute-done.6
  34.8 11.8 %collective-permute-start.1 = (f32[2,192,2,128]{3,1,2,0:T(8,128)S(1)}, f32[2,192,2,128]{3,1,2,0:T(8,128)S(1)}, u32[]{:S(2)}, u32[]{:S(2)}) collective-permute-start(f32[2,192,2,128]{3,1,2,0:T(8,128)S(1)} %bitcast_select_fusion), channel_id=1, source_target_pairs={{0,2},{1,3},{2,4},{3,5},{4,6},{5,7},{6,8},{7,9},{8,10},{9,11},{10,... | collective-permute-start | bytes 1179656 | tf_op jit(solution)/shard_map/ppermute | solution.py:14
  46.6 0.0 collective-permute-done.5
  46.6 18.8 %collective-permute-start = (f32[2,192,2,128]{3,1,2,0:T(8,128)S(1)}, f32[2,192,2,128]{3,1,2,0:T(8,128)S(1)}, u32[]{:S(2)}, u32[]{:S(2)}) collective-permute-start(f32[2,192,2,128]{3,1,2,0:T(8,128)S(1)} %bitcast_select_fusion), channel_id=1, source_target_pairs={{0,1},{1,2},{2,3},{3,4},{4,5},{5,6},{6,7},{7,8},{8,9},{9,10},{10,1... | collective-permute-start | bytes 1179656 | tf_op jit(solution)/shard_map/ppermute | solution.py:14
  65.4 0.0 copy-done.2
  65.5 0.0 collective-permute-done.4
  65.5 0.0 collective-permute-done.3
  65.5 0.0 collective-permute-done.2
  65.5 0.0 collective-permute-done.1
  65.5 1.2 collective-permute-done
  66.7 0.4 fusion.14
  67.2 0.6 fusion.43
  67.8 0.6 fusion.42
  68.3 0.6 fusion.11
  68.9 0.1 copy.72
  69.0 0.6 fusion.12
  69.6 0.1 copy.71
  69.8 0.8 copy.73
  70.6 33.8 %all-to-all-start = ((f32[16,2,192,8,2]{2,3,4,1,0:T(8,128)}), f32[16,2,192,8,2]{2,3,4,1,0:T(8,128)}, u32[]{:S(2)}, u32[]{:S(2)}) async-start(f32[16,2,192,8,2]{2,3,4,1,0:T(8,128)} %copy.73), calls=%async_computation | async-start | bytes 1048576 | tf_op jit(solution)/shard_map/all_to_all | solution.py:109
  104.4 0.0 copy-done
  104.4 4.4 %gather_fusion = f32[192,2,8,128]{3,0,2,1:T(8,128)S(1)} fusion(f32[2,8,192,128]{3,2,1,0:T(8,128)S(1)} %copy-done, s32[1024]{0:T(1024)S(1)} %pad_clamp_fusion), kind=kCustom, calls=%fused_computation | custom fusion | bytes 3146496 | tf_op jit(solution)/shard_map/jit(_take)/gather | solution.py:87
  108.8 0.5 fusion
  109.4 0.1 slice_bitcast_fusion.39
  109.5 0.1 copy.69
  109.5 0.1 copy.89
  109.6 0.1 copy.88
  109.7 0.1 copy.87
  109.7 0.1 copy.86
  109.8 0.1 copy.85
  109.9 0.1 copy.84
  109.9 0.1 copy.83
  110.0 0.1 copy.82
  110.1 0.1 copy.81
  110.2 0.1 copy.80
  110.2 0.1 copy.79
  110.3 0.1 copy.78
  110.4 0.1 copy.77
  110.4 0.1 copy.76
  110.5 0.1 copy.75
  110.6 3.8 %copy.106 = f32[1,8,2,192,192]{4,3,1,2,0:T(8,128)} copy(f32[1,8,2,192,192]{4,3,2,1,0:T(8,128)} %param.8) | data formatting | bytes 4718592 | tf_op args[3]
  114.4 4.5 %all-to-all-done = f32[16,2,192,8,2]{2,3,4,1,0:T(8,128)} async-done(((f32[16,2,192,8,2]{2,3,4,1,0:T(8,128)}), f32[16,2,192,8,2]{2,3,4,1,0:T(8,128)}, u32[]{:S(2)}, u32[]{:S(2)}) %all-to-all-start) | async-done | bytes 393248 | tf_op jit(solution)/shard_map/all_to_all | solution.py:109
  118.9 1.1 copy.74
  120.1 0.3 multiply_add_fusion
  120.4 0.3 multiply_subtract_fusion
  120.6 1.6 %copy-done.1 = f32[1,8,2,192,192]{4,3,1,2,0:T(8,128)S(1)} copy-done((f32[1,8,2,192,192]{4,3,1,2,0:T(8,128)S(1)}, f32[1,8,2,192,192]{4,3,1,2,0:T(8,128)}, u32[]{:S(2)}) %copy-start.1) | copy-done | bytes 2359320
  122.2 1.1 fusion.1
  123.4 1.1 fusion.2
  124.5 1.1 fusion.6
  125.6 1.1 fusion.10
  126.7 0.1 reshape.93
  126.8 0.2 reduce_sum.9
  127.0 0.6 multiply_bitcast_fusion
  (7 shorter events, 0.1 us)
Async XLA Ops:
  0.0 104.4 %copy-start = (f32[2,8,192,128]{3,2,1,0:T(8,128)S(1)}, f32[2,8,192,128]{3,2,1,0:T(8,128)}, u32[]{:S(2)}) copy-start(f32[2,8,192,128]{3,2,1,0:T(8,128)} %param.7) | copy-start | bytes 4718596
  1.5 63.9 %copy-start.2 = (f32[16,128]{1,0:T(8,128)S(1)}, f32[16,128]{1,0:T(8,128)}, u32[]{:S(2)}) copy-start(f32[16,128]{1,0:T(8,128)} %param.6) | copy-start | bytes 24580
  4.0 30.7 %collective-permute-start.6 = (f32[2,192,2,128]{3,1,2,0:T(8,128)S(1)}, f32[2,192,2,128]{3,1,2,0:T(8,128)S(1)}, u32[]{:S(2)}, u32[]{:S(2)}) collective-permute-start(f32[2,192,2,128]{3,1,2,0:T(8,128)S(1)} %bitcast_select_fusion), channel_id=1, source_target_pairs={{0,7},{1,8},{2,9},{3,10},{4,11},{5,12},{6,13},{7,14},{8,15},{16,23... | collective-permute-start | bytes 1179656 | tf_op jit(solution)/shard_map/ppermute | solution.py:14
  9.4 37.2 %collective-permute-start.5 = (f32[2,192,2,128]{3,1,2,0:T(8,128)S(1)}, f32[2,192,2,128]{3,1,2,0:T(8,128)S(1)}, u32[]{:S(2)}, u32[]{:S(2)}) collective-permute-start(f32[2,192,2,128]{3,1,2,0:T(8,128)S(1)} %bitcast_select_fusion), channel_id=1, source_target_pairs={{0,6},{1,7},{2,8},{3,9},{4,10},{5,11},{6,12},{7,13},{8,14},{9,15},... | collective-permute-start | bytes 1179656 | tf_op jit(solution)/shard_map/ppermute | solution.py:14
  13.9 17.6 %collective-permute-start.7 = (f32[2,192,1,128]{3,1,2,0:T(8,128)S(1)}, f32[2,192,1,128]{3,1,2,0:T(8,128)S(1)}, u32[]{:S(2)}, u32[]{:S(2)}) collective-permute-start(f32[2,192,1,128]{3,1,2,0:T(8,128)S(1)} %slice.303), channel_id=1, source_target_pairs={{0,8},{1,9},{2,10},{3,11},{4,12},{5,13},{6,14},{7,15},{16,24},{17,... | collective-permute-start | bytes 589832 | tf_op jit(solution)/shard_map/ppermute | solution.py:14
  15.8 49.6 %collective-permute-start.4 = (f32[2,192,2,128]{3,1,2,0:T(8,128)S(1)}, f32[2,192,2,128]{3,1,2,0:T(8,128)S(1)}, u32[]{:S(2)}, u32[]{:S(2)}) collective-permute-start(f32[2,192,2,128]{3,1,2,0:T(8,128)S(1)} %bitcast_select_fusion), channel_id=1, source_target_pairs={{0,5},{1,6},{2,7},{3,8},{4,9},{5,10},{6,11},{7,12},{8,13},{9,14},{... | collective-permute-start | bytes 1179656 | tf_op jit(solution)/shard_map/ppermute | solution.py:14
  17.2 48.3 %collective-permute-start.3 = (f32[2,192,2,128]{3,1,2,0:T(8,128)S(1)}, f32[2,192,2,128]{3,1,2,0:T(8,128)S(1)}, u32[]{:S(2)}, u32[]{:S(2)}) collective-permute-start(f32[2,192,2,128]{3,1,2,0:T(8,128)S(1)} %bitcast_select_fusion), channel_id=1, source_target_pairs={{0,4},{1,5},{2,6},{3,7},{4,8},{5,9},{6,10},{7,11},{8,12},{9,13},{1... | collective-permute-start | bytes 1179656 | tf_op jit(solution)/shard_map/ppermute | solution.py:14
  31.5 34.0 %collective-permute-start.2 = (f32[2,192,2,128]{3,1,2,0:T(8,128)S(1)}, f32[2,192,2,128]{3,1,2,0:T(8,128)S(1)}, u32[]{:S(2)}, u32[]{:S(2)}) collective-permute-start(f32[2,192,2,128]{3,1,2,0:T(8,128)S(1)} %bitcast_select_fusion), channel_id=1, source_target_pairs={{0,3},{1,4},{2,5},{3,6},{4,7},{5,8},{6,9},{7,10},{8,11},{9,12},{10... | collective-permute-start | bytes 1179656 | tf_op jit(solution)/shard_map/ppermute | solution.py:14
  34.8 30.7 %collective-permute-start.1 = (f32[2,192,2,128]{3,1,2,0:T(8,128)S(1)}, f32[2,192,2,128]{3,1,2,0:T(8,128)S(1)}, u32[]{:S(2)}, u32[]{:S(2)}) collective-permute-start(f32[2,192,2,128]{3,1,2,0:T(8,128)S(1)} %bitcast_select_fusion), channel_id=1, source_target_pairs={{0,2},{1,3},{2,4},{3,5},{4,6},{5,7},{6,8},{7,9},{8,10},{9,11},{10,... | collective-permute-start | bytes 1179656 | tf_op jit(solution)/shard_map/ppermute | solution.py:14
  46.6 20.1 %collective-permute-start = (f32[2,192,2,128]{3,1,2,0:T(8,128)S(1)}, f32[2,192,2,128]{3,1,2,0:T(8,128)S(1)}, u32[]{:S(2)}, u32[]{:S(2)}) collective-permute-start(f32[2,192,2,128]{3,1,2,0:T(8,128)S(1)} %bitcast_select_fusion), channel_id=1, source_target_pairs={{0,1},{1,2},{2,3},{3,4},{4,5},{5,6},{6,7},{7,8},{8,9},{9,10},{10,1... | collective-permute-start | bytes 1179656 | tf_op jit(solution)/shard_map/ppermute | solution.py:14
  70.6 48.3 %all-to-all-start = ((f32[16,2,192,8,2]{2,3,4,1,0:T(8,128)}), f32[16,2,192,8,2]{2,3,4,1,0:T(8,128)}, u32[]{:S(2)}, u32[]{:S(2)}) async-start(f32[16,2,192,8,2]{2,3,4,1,0:T(8,128)} %copy.73), calls=%async_computation | async-start | bytes 1048576 | tf_op jit(solution)/shard_map/all_to_all | solution.py:109
  120.4 1.9 %copy-start.1 = (f32[1,8,2,192,192]{4,3,1,2,0:T(8,128)S(1)}, f32[1,8,2,192,192]{4,3,1,2,0:T(8,128)}, u32[]{:S(2)}) copy-start(f32[1,8,2,192,192]{4,3,1,2,0:T(8,128)} %copy.106) | copy-start | bytes 7077892
where the time goes:
time: 128 us
  starting transfers between devices  82.3 us (64%)
  waiting for transfers between devices  18.5 us (14%)
  local copies, waits for them, and re-layouts  15.8 us (12%)
  matrix products  6.71 us (5%)
  other arithmetic  3.93 us (3%)
    ppermute x8, starting transfers between devices, shifted(): lax.ppermute(value, axis, [(source, source + steps) for source in range(l...  48.5 us
    all_to_all x1, starting transfers between devices, body(): lax.all_to_all(pieces, 'band', split_axis=0, concat_axis=4, tiled=True)[0]  33.8 us
    ppermute x8, waiting for transfers between devices, shifted(): lax.ppermute(value, axis, [(source, source + steps) for source in range(l...  14 us
    unnamed x7, local copies, waits for them, and re-layouts  5.42 us
    all_to_all x1, waiting for transfers between devices, body(): lax.all_to_all(pieces, 'band', split_axis=0, concat_axis=4, tiled=True)[0]  4.54 us
    dot_general x4, matrix products, contract(): jnp.einsum('qds,dqf->qsf', weight_part, field_part, precision=highest)  4.45 us
    gather x1, local copies, waits for them, and re-layouts, body(): taps_ordered = jnp.take(dish_filter, dish_order, axis=2)  4.4 us
  transfers between devices with their start and end apart: 9, of which 3 were waited for; matrix products, arithmetic and copies ran while one was open for 8% of the time, Pallas kernels for 0%

commit v1 on v0

v1 whole, which is shorter than its diff:
```python
import functools
import math

import jax
import jax.numpy as jnp
import ml_dtypes
import numpy as np
from jax import lax
from jax.experimental import pallas as pl
from jax.experimental.pallas import tpu as pltpu
from jax.sharding import PartitionSpec as P

INTEG = 4
CHUNK = 32
F32 = jnp.float32
BF16 = jnp.bfloat16


def split(value):
    high = value.astype(BF16)
    return high, (value - high.astype(F32)).astype(BF16)


def dot(lhs, rhs):
    return jnp.dot(lhs, rhs, preferred_element_type=F32)


def dot3(lhs, rhs):
    return dot(lhs[0], rhs[0]) + (dot(lhs[0], rhs[1]) + dot(lhs[1], rhs[0]))


def fourier_matrix(length):
    counter = np.arange(length)
    angles = (counter[:, None] * counter[None, :] % length) * (2.0 * math.pi / length)
    cosine = np.cos(angles) / math.sqrt(length)
    sine = np.sin(angles) / math.sqrt(length)
    full = np.block([[cosine, -sine], [sine, cosine]]).astype(np.float32)
    high = full.astype(ml_dtypes.bfloat16)
    low = (full - high.astype(np.float32)).astype(ml_dtypes.bfloat16)
    return np.stack([high, low])


def kernel(
    dims,
    x_ref,
    proto_ref,
    order_ref,
    fourier_hbm,
    taps_hbm,
    weights_hbm,
    out_ref,
    stage,
    voltages,
    spectra,
    filtered,
    turned,
    panels,
    fourier,
    taps,
    weights,
    beams_high,
    beams_low,
    load_sems,
    sems,
):
    devices, workers, group, slice_frames, frames, owners = dims
    pfb = proto_ref.shape[0]
    chan = proto_ref.shape[1]
    fir = taps.shape[1]
    dishes = order_ref.shape[1]
    band_chans, _, _, beams = weights.shape
    pairs = group // 2
    chunks = frames // CHUNK
    half = workers * pairs
    me = lax.axis_index("band")
    worker = (me * workers + devices - 1) // devices
    active = jnp.logical_and(worker < workers, worker * devices // workers == me)
    worker = jnp.minimum(worker, workers - 1)
    dish_start = pl.multiple_of(worker * group, group)

    load_weights = pltpu.make_async_copy(weights_hbm.at[0], weights, load_sems.at[0])
    load_taps = pltpu.make_async_copy(
        taps_hbm.at[:, :, pl.ds(dish_start, group), :], taps, load_sems.at[1]
    )
    load_fourier = pltpu.make_async_copy(fourier_hbm, fourier, load_sems.at[2])

    barrier = pltpu.get_barrier_semaphore()

    @pl.loop(1, devices)
    def _(step):
        pl.semaphore_signal(barrier, inc=1, device_id={"band": lax.rem(me + step, devices)})

    load_weights.start()
    load_taps.start()
    load_fourier.start()
    for target in range(workers):
        for frame in range(slice_frames):
            for part in range(2):
                stage[target, frame, part] = x_ref[
                    part,
                    target * group : (target + 1) * group,
                    frame * chan : (frame + 1) * chan,
                ]
    pl.semaphore_wait(barrier, devices - 1)

    arrival = pl.ds(pfb - 1 + me * slice_frames, slice_frames)

    @pl.loop(0, workers)
    def _(step):
        target = lax.rem(worker + step, workers)
        device = target * devices // workers

        @pl.when(device != me)
        def _():
            pltpu.make_async_remote_copy(
                src_ref=stage.at[target],
                dst_ref=voltages.at[arrival],
                send_sem=sems.at[0],
                recv_sem=sems.at[1],
                device_id={"band": device},
            ).start()

        @pl.when(device == me)
        def _():
            pltpu.make_async_copy(stage.at[target], voltages.at[arrival], sems.at[1]).start()

    row = lax.broadcasted_iota(jnp.int32, (dishes, dishes), 0)
    dish_of_row = jnp.where(row < half, 2 * row, 2 * (row - half) + 1)
    chosen = jnp.where(order_ref[...] == dish_of_row, 1.0, 0.0).astype(BF16)
    load_weights.wait()

    @pl.loop(0, band_chans)
    def _(index):
        for part in range(2):
            high, low = split(weights[index, part])
            rows = slice(part * beams, (part + 1) * beams)
            beams_high[index, rows, :] = dot(chosen, high).T.astype(BF16)
            beams_low[index, rows, :] = dot(chosen, low).T.astype(BF16)

    load_taps.wait()
    load_fourier.wait()

    @pl.when(active)
    def _():
        voltages[0 : pfb - 1] = jnp.zeros((pfb - 1, 2, group, chan), F32)
        spectra[:, 0 : fir - 1] = jnp.zeros((2, fir - 1, group, chan), F32)
        landed = voltages.at[pl.ds(pfb - 1, frames)]
        pltpu.make_async_copy(landed, landed, sems.at[1]).wait()
        step_frames = 8

        @pl.loop(0, frames // step_frames)
        def _(step):
            first = step * step_frames
            pieces = []
            for part in range(2):
                total = jnp.zeros((step_frames, group, chan), F32)
                for tap in range(pfb):
                    total = total + proto_ref[tap : tap + 1, :] * voltages[
                        pl.ds(first + pfb - 1 - tap, step_frames), part
                    ]
                pieces.append(total.reshape(step_frames * group, chan))
            lhs = split(jnp.concatenate(pieces, axis=1))
            result = dot3(lhs, (fourier[0], fourier[1]))
            for part in range(2):
                spectra[part, pl.ds(first + fir - 1, step_frames)] = result[
                    :, part * chan : (part + 1) * chan
                ].reshape(step_frames, group, chan)

        @pl.loop(0, frames // step_frames)
        def _(step):
            first = step * step_frames
            out_real = jnp.zeros((step_frames, group, chan), F32)
            out_imag = jnp.zeros((step_frames, group, chan), F32)
            for tap in range(fir):
                window = pl.ds(first + fir - 1 - tap, step_frames)
                part_real = spectra[0, window]
                part_imag = spectra[1, window]
                out_real = out_real + taps[0, tap] * part_real - taps[1, tap] * part_imag
                out_imag = out_imag + taps[0, tap] * part_imag + taps[1, tap] * part_real
            rows = pl.ds(pl.multiple_of(first * group, group), step_frames * group)
            filtered[0, rows, :] = out_real.reshape(step_frames * group, chan)
            filtered[1, rows, :] = out_imag.reshape(step_frames * group, chan)

        for chunk in range(chunks):
            for pair in range(pairs):
                tile = [
                    filtered[part, pl.ds(chunk * CHUNK * group + dish, CHUNK, stride=group), :]
                    for dish in (2 * pair, 2 * pair + 1)
                    for part in range(2)
                ]
                turned[chunk, pair] = jnp.concatenate(tile, axis=0).T

        @pl.loop(0, devices)
        def _(step):
            device = lax.rem(me + step, devices)
            start = pl.multiple_of(device // owners * band_chans, band_chans)
            source = turned.at[:, :, pl.ds(start, band_chans), :]

            @pl.when(device != me)
            def _():
                pltpu.make_async_remote_copy(
                    src_ref=source,
                    dst_ref=panels.at[:, worker],
                    send_sem=sems.at[2],
                    recv_sem=sems.at[3],
                    device_id={"band": device},
                ).start()

            @pl.when(device == me)
            def _():
                pltpu.make_async_copy(source, panels.at[:, worker], sems.at[3]).start()

    pltpu.make_async_copy(panels, panels, sems.at[3]).wait()

    lane_b = lax.broadcasted_iota(jnp.int32, (beams, 4 * CHUNK), 1)
    per_chunk = CHUNK // INTEG
    columns = per_chunk * chunks
    from_lane = lax.broadcasted_iota(jnp.int32, (4 * CHUNK, columns), 0)
    to_column = lax.broadcasted_iota(jnp.int32, (4 * CHUNK, columns), 1)
    in_part = jnp.where(from_lane < CHUNK, from_lane, from_lane - CHUNK)
    flat = panels.reshape(chunks, half * band_chans, 4 * CHUNK)
    for index in range(band_chans):
        power = jnp.zeros((beams, columns), F32)
        lhs = (beams_high[index], beams_low[index])
        for chunk in range(chunks):
            field = flat[chunk, pl.ds(index, half, stride=band_chans), :]
            both = jnp.concatenate([field, pltpu.roll(field, 2 * CHUNK, 1)], axis=0)
            product = dot3(lhs, split(both))
            upper = product[:beams]
            lower = product[beams:]
            crossed = jnp.where(
                lane_b < CHUNK,
                -pltpu.roll(lower, 3 * CHUNK, 1),
                pltpu.roll(lower, CHUNK, 1),
            )
            beam = upper + crossed
            energy = split(beam * beam)
            pick = jnp.logical_and(
                from_lane < 2 * CHUNK, in_part // INTEG + per_chunk * chunk == to_column
            )
            mean = jnp.where(pick, 1.0 / INTEG, 0.0).astype(BF16)
            power = power + (dot(energy[0], mean) + dot(energy[1], mean))
        out_ref[0, index] = power

    @pl.when(active)
    def _():
        sent = stage.at[pl.ds(0, workers - 1)]
        pltpu.make_async_copy(sent, sent, sems.at[0]).wait()
        for _ in range(owners - 1):
            pltpu.make_async_copy(turned, turned, sems.at[2]).wait()
        rest = turned.at[:, :, pl.ds(0, chan - band_chans), :]
        pltpu.make_async_copy(rest, rest, sems.at[2]).wait()

    @pl.when(jnp.logical_not(active))
    def _():
        pltpu.make_async_copy(stage, stage, sems.at[0]).wait()


def body(devices, samples, prototype, dish_filter, beam_weights, dish_order):
    pfb, chan = prototype.shape
    fir, dishes = dish_filter.shape[1:3]
    band_chans, _, _, beams = beam_weights.shape[1:]
    owners = devices // (chan // band_chans)
    slice_frames = samples.shape[2] // chan
    frames = slice_frames * devices
    group = 8 * (-(-dishes // (8 * devices)))
    workers = dishes // group
    chunks = frames // CHUNK
    pairs = group // 2
    dims = (devices, workers, group, slice_frames, frames, owners)
    any_spec = pl.BlockSpec(memory_space=pl.ANY)
    vmem_spec = pl.BlockSpec(memory_space=pltpu.VMEM)
    return pl.pallas_call(
        functools.partial(kernel, dims),
        out_shape=jax.ShapeDtypeStruct((1, band_chans, beams, frames // INTEG), F32),
        in_specs=[vmem_spec, vmem_spec, vmem_spec, any_spec, any_spec, any_spec],
        out_specs=vmem_spec,
        scratch_shapes=[
            pltpu.VMEM((workers, slice_frames, 2, group, chan), F32),
            pltpu.VMEM((pfb - 1 + frames, 2, group, chan), F32),
            pltpu.VMEM((2, fir - 1 + frames, group, chan), F32),
            pltpu.VMEM((2, frames * group, chan), F32),
            pltpu.VMEM((chunks, pairs, chan, 4 * CHUNK), F32),
            pltpu.VMEM((chunks, workers, pairs, band_chans, 4 * CHUNK), F32),
            pltpu.VMEM((2, 2 * chan, 2 * chan), BF16),
            pltpu.VMEM((2, fir, group, chan), F32),
            pltpu.VMEM((band_chans, 2, dishes, beams), F32),
            pltpu.VMEM((band_chans, 2 * beams, dishes), BF16),
            pltpu.VMEM((band_chans, 2 * beams, dishes), BF16),
            pltpu.SemaphoreType.DMA((3,)),
            pltpu.SemaphoreType.DMA((4,)),
        ],
        compiler_params=pltpu.CompilerParams(
            collective_id=0, has_side_effects=True, vmem_limit_bytes=48 * 2**20
        ),
    )(
        samples,
        prototype,
        dish_order.reshape(1, dishes),
        jnp.asarray(fourier_matrix(chan)),
        dish_filter,
        beam_weights,
    )


def solution(mesh):
    placed = (P(None, None, ("grp", "band")), P(), P(), P("band", None, None, None, None), P())
    return jax.shard_map(
        functools.partial(body, mesh.shape["band"]),
        mesh=mesh,
        in_specs=placed,
        out_specs=P(("grp", "band"), None, None, None),
        check_vma=False,
    )
```

time: 128 us -> 39.3 us (0.31)
  the two profiles are of different devices: /device:TPU:0 before, /device:TPU:29 now
where the time goes in v1:
time: 39.3 us; the launch traced here: 39 us
  Pallas kernels  31.4 us (80%)
  local copies, waits for them, and re-layouts  7.55 us (19%)
    pallas_call x1, Pallas kernels, body(): pl.pallas_call(functools.partial(kernel, dims), out_shape=jax.ShapeDtypeS...  31.4 us
    unnamed x12, local copies, waits for them, and re-layouts  6.62 us
    pallas_call x1, local copies, waits for them, and re-layouts, body(): pl.pallas_call(functools.partial(kernel, dims), out_shape=jax.ShapeDtypeS...  0.93 us

profile of v1, /device:TPU:29, one launch (start us, length us, event | category | flops | bytes accessed | tf_op | source)
XLA Modules:
  0.0 39.0 jit_solution(11501632950604066119)
XLA Ops:
  0.0 0.0 copy-start
  0.0 1.9 %copy-done = f32[1,8,2,192,192]{4,3,2,1,0:T(8,128)S(1)} copy-done((f32[1,8,2,192,192]{4,3,2,1,0:T(8,128)S(1)}, f32[1,8,2,192,192]{4,3,2,1,0:T(8,128)}, u32[]{:S(2)}) %copy-start) | copy-done | bytes 2359320
  1.9 0.0 copy-start.1
  1.9 1.4 %copy-done.1 = f32[2,8,192,128]{3,2,1,0:T(8,128)S(1)} copy-done((f32[2,8,192,128]{3,2,1,0:T(8,128)S(1)}, f32[2,8,192,128]{3,2,1,0:T(8,128)}, u32[]{:S(2)}) %copy-start.1) | copy-done | bytes 1572888
  3.3 0.0 copy-start.2
  3.3 1.0 %copy-done.2 = f32[2,192,256]{2,1,0:T(8,128)S(1)} copy-done((f32[2,192,256]{2,1,0:T(8,128)S(1)}, f32[2,192,256]{2,1,0:T(8,128)}, u32[]{:S(2)}) %copy-start.2) | copy-done | bytes 393240
  4.3 0.0 copy-start.3
  4.3 0.9 %copy-done.3 = bf16[2,256,256]{2,1,0:T(8,128)(2,1)S(1)} copy-done((bf16[2,256,256]{2,1,0:T(8,128)(2,1)S(1)}, bf16[2,256,256]{2,1,0:T(8,128)(2,1)}, u32[]{:S(2)}) %copy-start.3) | copy-done | bytes 262168
  5.2 0.0 copy-start.4
  5.2 0.7 %copy-done.4 = f32[16,128]{1,0:T(8,128)S(1)} copy-done((f32[16,128]{1,0:T(8,128)S(1)}, f32[16,128]{1,0:T(8,128)}, u32[]{:S(2)}) %copy-start.4) | copy-done | bytes 8216
  5.9 0.0 copy-start.5
  5.9 0.7 %copy-done.5 = s32[192]{0:T(256)S(1)} copy-done((s32[192]{0:T(256)S(1)}, s32[192]{0:T(256)}, u32[]{:S(2)}) %copy-start.5) | copy-done | bytes 792
  6.6 31.4 %shard_map.64 = f32[1,8,192,8]{3,2,1,0:T(8,128)S(1)} custom-call(f32[2,192,256]{2,1,0:T(8,128)S(1)} %copy-done.2, f32[16,128]{1,0:T(8,128)S(1)} %copy-done.4, s32[1,192]{1,0:T(1,128)S(1)} %bitcast.1, bf16[2,256,256]{2,1,0:T(8,128)(2,1)S(1)} %copy-done.3, f32[2,8,192,128]{3,2,1,0:T(8,128)S(1)} %copy-done.1, f32[1,8,2,192,192]{4,3,2,1,0:T(8,128)S(1)} %copy-done), custom_call_target="tpu_custom_call" | custom-call | tf_op jit(solution)/shard_map/pallas_call | solution.py:273
  38.0 0.9 %copy.7 = f32[1,8,192,8]{2,3,1,0:T(8,128)} copy(f32[1,8,192,8]{3,2,1,0:T(8,128)S(1)} %shard_map.64) | data formatting | bytes 98304 | tf_op jit(solution)/shard_map/pallas_call | solution.py:273
Async XLA Ops:
  0.0 1.9 %copy-start = (f32[1,8,2,192,192]{4,3,2,1,0:T(8,128)S(1)}, f32[1,8,2,192,192]{4,3,2,1,0:T(8,128)}, u32[]{:S(2)}) copy-start(f32[1,8,2,192,192]{4,3,2,1,0:T(8,128)} %weights_hbm.1) | copy-start | bytes 7077892
  1.9 1.4 %copy-start.1 = (f32[2,8,192,128]{3,2,1,0:T(8,128)S(1)}, f32[2,8,192,128]{3,2,1,0:T(8,128)}, u32[]{:S(2)}) copy-start(f32[2,8,192,128]{3,2,1,0:T(8,128)} %taps_hbm.1) | copy-start | bytes 4718596
  3.3 1.0 %copy-start.2 = (f32[2,192,256]{2,1,0:T(8,128)S(1)}, f32[2,192,256]{2,1,0:T(8,128)}, u32[]{:S(2)}) copy-start(f32[2,192,256]{2,1,0:T(8,128)} %x_ref.1) | copy-start | bytes 1179652
  4.3 0.9 %copy-start.3 = (bf16[2,256,256]{2,1,0:T(8,128)(2,1)S(1)}, bf16[2,256,256]{2,1,0:T(8,128)(2,1)}, u32[]{:S(2)}) copy-start(bf16[2,256,256]{2,1,0:T(8,128)(2,1)} %constant.2.clone.fourier_hbm) | copy-start | bytes 786436
  5.2 0.7 %copy-start.4 = (f32[16,128]{1,0:T(8,128)S(1)}, f32[16,128]{1,0:T(8,128)}, u32[]{:S(2)}) copy-start(f32[16,128]{1,0:T(8,128)} %proto_ref.1) | copy-start | bytes 24580
  5.9 0.7 %copy-start.5 = (s32[192]{0:T(256)S(1)}, s32[192]{0:T(256)}, u32[]{:S(2)}) copy-start(s32[192]{0:T(256)} %param.10) | copy-start | bytes 2308

commit v2 on v1

v2 whole, which is shorter than its diff:
```python
import functools
import math

import jax
import jax.numpy as jnp
import ml_dtypes
import numpy as np
from jax import lax
from jax.experimental import pallas as pl
from jax.experimental.pallas import tpu as pltpu
from jax.sharding import PartitionSpec as P

INTEG = 4
CHUNK = 32
SUB = 8
F32 = jnp.float32
BF16 = jnp.bfloat16


def split(value):
    high = value.astype(BF16)
    return high, (value - high.astype(F32)).astype(BF16)


def dot(lhs, rhs):
    return jnp.dot(lhs, rhs, preferred_element_type=F32)


def dot3(lhs, rhs):
    return dot(lhs[0], rhs[0]) + (dot(lhs[0], rhs[1]) + dot(lhs[1], rhs[0]))


def fourier_matrix(length):
    counter = np.arange(length)
    angles = (counter[:, None] * counter[None, :] % length) * (2.0 * math.pi / length)
    cosine = np.cos(angles) / math.sqrt(length)
    sine = np.sin(angles) / math.sqrt(length)
    full = np.block([[cosine, -sine], [sine, cosine]]).astype(np.float32)
    high = full.astype(ml_dtypes.bfloat16)
    low = (full - high.astype(np.float32)).astype(ml_dtypes.bfloat16)
    return np.stack([high, low])


def kernel(
    dims,
    x_hbm,
    proto_hbm,
    order_hbm,
    fourier_hbm,
    taps_hbm,
    weights_hbm,
    out_ref,
    stage,
    voltages,
    spectra,
    filtered,
    turned,
    panels,
    proto_ref,
    order_ref,
    fourier,
    taps,
    weights,
    beams_high,
    beams_low,
    partial,
    load_sems,
    send_sems,
    voltage_sems,
    panel_sems,
):
    devices, workers, group, slice_frames, frames, owners = dims
    pfb = proto_ref.shape[0]
    chan = proto_ref.shape[1]
    fir = taps.shape[1]
    dishes = order_ref.shape[1]
    band_chans, _, _, beams = weights.shape
    halves = group // SUB
    pairs = SUB // 2
    chunks = frames // CHUNK
    rows_half = workers * pairs
    me = lax.axis_index("band")
    worker = (me * workers + devices - 1) // devices
    active = jnp.logical_and(worker < workers, worker * devices // workers == me)
    worker = jnp.minimum(worker, workers - 1)
    dish_start = pl.multiple_of(worker * group, group)

    load_weights = pltpu.make_async_copy(weights_hbm.at[0], weights, load_sems.at[5])
    load_taps = pltpu.make_async_copy(
        taps_hbm.at[:, :, pl.ds(dish_start, group), :], taps, load_sems.at[1]
    )
    load_fourier = pltpu.make_async_copy(fourier_hbm, fourier, load_sems.at[2])

    load_order = pltpu.make_async_copy(order_hbm, order_ref, load_sems.at[3])
    load_proto = pltpu.make_async_copy(proto_hbm, proto_ref, load_sems.at[4])
    for frame in range(slice_frames):
        pltpu.make_async_copy(
            x_hbm.at[:, :, frame * chan : (frame + 1) * chan], stage.at[frame], load_sems.at[0]
        ).start()

    barrier = pltpu.get_barrier_semaphore()

    @pl.loop(1, devices)
    def _(step):
        pl.semaphore_signal(barrier, inc=1, device_id={"band": lax.rem(me + step, devices)})

    load_order.start()
    load_proto.start()
    load_weights.start()
    load_taps.start()
    load_fourier.start()
    pltpu.make_async_copy(stage, stage, load_sems.at[0]).wait()
    pl.semaphore_wait(barrier, devices - 1)

    arrival = pl.ds(pfb - 1 + me * slice_frames, slice_frames)

    for half in range(halves):

        @pl.loop(0, workers)
        def _(step):
            target = lax.rem(worker + step, workers)
            device = target * devices // workers
            start = pl.multiple_of(target * group + half * SUB, SUB)
            outgoing = stage.at[:, :, pl.ds(start, SUB), :]
            landing = voltages.at[half, arrival]

            @pl.when(device != me)
            def _():
                pltpu.make_async_remote_copy(
                    src_ref=outgoing,
                    dst_ref=landing,
                    send_sem=send_sems.at[0],
                    recv_sem=voltage_sems.at[half],
                    device_id={"band": device},
                ).start()

            @pl.when(device == me)
            def _():
                pltpu.make_async_copy(outgoing, landing, voltage_sems.at[half]).start()

    load_order.wait()
    row = lax.broadcasted_iota(jnp.int32, (dishes, dishes), 0)
    dish_of_row = jnp.zeros((dishes, dishes), jnp.int32)
    for block in range(2 * halves):
        rest = row - block * rows_half
        dish = rest // pairs * group + rest % pairs * 2 + block // 2 * SUB + block % 2
        dish_of_row = jnp.where(rest >= 0, dish, dish_of_row)
    chosen = jnp.where(order_ref[...] == dish_of_row, 1.0, 0.0).astype(BF16)
    load_weights.wait()

    @pl.loop(0, band_chans)
    def _(index):
        for part in range(2):
            high, low = split(weights[index, part])
            beams_high[index, part] = dot(chosen, high).astype(BF16)
            beams_low[index, part] = dot(chosen, low).astype(BF16)

    load_proto.wait()
    load_taps.wait()
    load_fourier.wait()

    @pl.when(active)
    def _():
        spectra[:, 0 : fir - 1] = jnp.zeros((2, fir - 1, SUB, chan), F32)
        for half in range(halves):
            voltages[half, 0 : pfb - 1] = jnp.zeros((pfb - 1, 2, SUB, chan), F32)
        step_frames = 16
        for half in range(halves):
            landed = voltages.at[half, pl.ds(pfb - 1, frames)]
            pltpu.make_async_copy(landed, landed, voltage_sems.at[half]).wait()

            @pl.loop(0, frames // step_frames)
            def _(step):
                first = step * step_frames
                pieces = []
                for part in range(2):
                    total = jnp.zeros((step_frames, SUB, chan), F32)
                    for tap in range(pfb):
                        total = total + proto_ref[tap : tap + 1, :] * voltages[
                            half, pl.ds(first + pfb - 1 - tap, step_frames), part
                        ]
                    pieces.append(total.reshape(step_frames * SUB, chan))
                lhs = split(jnp.concatenate(pieces, axis=1))
                result = dot3(lhs, (fourier[0], fourier[1]))
                for part in range(2):
                    spectra[part, pl.ds(first + fir - 1, step_frames)] = result[
                        :, part * chan : (part + 1) * chan
                    ].reshape(step_frames, SUB, chan)

            @pl.loop(0, frames // step_frames)
            def _(step):
                first = step * step_frames
                out_real = jnp.zeros((step_frames, SUB, chan), F32)
                out_imag = jnp.zeros((step_frames, SUB, chan), F32)
                for tap in range(fir):
                    window = pl.ds(first + fir - 1 - tap, step_frames)
                    part_real = spectra[0, window]
                    part_imag = spectra[1, window]
                    tap_real = taps[0, tap, half * SUB : (half + 1) * SUB]
                    tap_imag = taps[1, tap, half * SUB : (half + 1) * SUB]
                    out_real = out_real + tap_real * part_real - tap_imag * part_imag
                    out_imag = out_imag + tap_real * part_imag + tap_imag * part_real
                rows = pl.ds(pl.multiple_of(first * SUB, SUB), step_frames * SUB)
                filtered[0, rows, :] = out_real.reshape(step_frames * SUB, chan)
                filtered[1, rows, :] = out_imag.reshape(step_frames * SUB, chan)

            for chunk in range(chunks):
                for pair in range(pairs):
                    tile = [
                        filtered[part, pl.ds(chunk * CHUNK * SUB + dish, CHUNK, stride=SUB), :]
                        for dish in (2 * pair, 2 * pair + 1)
                        for part in range(2)
                    ]
                    turned[half, chunk, pair] = jnp.concatenate(tile, axis=0).T

            @pl.loop(0, devices)
            def _(step):
                device = lax.rem(me + step, devices)
                start = pl.multiple_of(device // owners * band_chans, band_chans)
                source = turned.at[half, :, :, pl.ds(start, band_chans), :]
                landing = panels.at[half, :, worker]

                @pl.when(device != me)
                def _():
                    pltpu.make_async_remote_copy(
                        src_ref=source,
                        dst_ref=landing,
                        send_sem=send_sems.at[1],
                        recv_sem=panel_sems.at[half],
                        device_id={"band": device},
                    ).start()

                @pl.when(device == me)
                def _():
                    pltpu.make_async_copy(source, landing, panel_sems.at[half]).start()

    per_chunk = CHUNK // INTEG
    from_frame = lax.broadcasted_iota(jnp.int32, (per_chunk, CHUNK), 1)
    to_sample = lax.broadcasted_iota(jnp.int32, (per_chunk, CHUNK), 0)
    mean = jnp.where(from_frame // INTEG == to_sample, 1.0 / INTEG, 0.0).astype(BF16)
    flat = panels.reshape(halves, chunks, rows_half * band_chans, 4 * CHUNK)
    for half in range(halves):
        pltpu.make_async_copy(panels.at[half], panels.at[half], panel_sems.at[half]).wait()
        depth = slice(2 * half * rows_half, 2 * (half + 1) * rows_half)
        for index in range(band_chans):
            for chunk in range(chunks):
                field = flat[half, chunk, pl.ds(index, rows_half, stride=band_chans), :]
                both = jnp.concatenate([field, pltpu.roll(field, 2 * CHUNK, 1)], axis=0)
                high, low = split(both.T[: 2 * CHUNK])
                stacked = jnp.concatenate([high, low], axis=0)
                products = []
                for part in range(2):
                    wide = dot(stacked, beams_high[index, part, depth, :])
                    total = wide[: 2 * CHUNK] + (
                        wide[2 * CHUNK :] + dot(high, beams_low[index, part, depth, :])
                    )
                    if half > 0:
                        total = total + partial[index, chunk, part]
                    if half < halves - 1:
                        partial[index, chunk, part] = total
                    products.append(total)
                if half == halves - 1:
                    real = products[0][:CHUNK] - products[1][CHUNK:]
                    imag = products[0][CHUNK:] + products[1][:CHUNK]
                    energy = split(real * real + imag * imag)
                    out_ref[0, index, chunk * per_chunk : (chunk + 1) * per_chunk, :] = dot(
                        mean, energy[0]
                    ) + dot(mean, energy[1])

    @pl.when(active)
    def _():
        sent = stage.at[:, :, pl.ds(0, dishes - group), :]
        pltpu.make_async_copy(sent, sent, send_sems.at[0]).wait()
        for _ in range(owners - 1):
            pltpu.make_async_copy(turned, turned, send_sems.at[1]).wait()
        rest = turned.at[:, :, :, pl.ds(0, chan - band_chans), :]
        pltpu.make_async_copy(rest, rest, send_sems.at[1]).wait()

    @pl.when(jnp.logical_not(active))
    def _():
        pltpu.make_async_copy(stage, stage, send_sems.at[0]).wait()


def body(devices, samples, prototype, dish_filter, beam_weights, dish_order):
    pfb, chan = prototype.shape
    fir, dishes = dish_filter.shape[1:3]
    band_chans, _, _, beams = beam_weights.shape[1:]
    owners = devices // (chan // band_chans)
    slice_frames = samples.shape[2] // chan
    frames = slice_frames * devices
    group = SUB * (-(-dishes // (SUB * devices)))
    workers = dishes // group
    chunks = frames // CHUNK
    halves = group // SUB
    pairs = SUB // 2
    dims = (devices, workers, group, slice_frames, frames, owners)
    hbm_spec = pl.BlockSpec(memory_space=pltpu.HBM)
    vmem_spec = pl.BlockSpec(memory_space=pltpu.VMEM)
    power = pl.pallas_call(
        functools.partial(kernel, dims),
        out_shape=jax.ShapeDtypeStruct((1, band_chans, frames // INTEG, beams), F32),
        in_specs=[hbm_spec] * 6,
        out_specs=vmem_spec,
        scratch_shapes=[
            pltpu.VMEM((slice_frames, 2, dishes, chan), F32),
            pltpu.VMEM((halves, pfb - 1 + frames, 2, SUB, chan), F32),
            pltpu.VMEM((2, fir - 1 + frames, SUB, chan), F32),
            pltpu.VMEM((2, frames * SUB, chan), F32),
            pltpu.VMEM((halves, chunks, pairs, chan, 4 * CHUNK), F32),
            pltpu.VMEM((halves, chunks, workers, pairs, band_chans, 4 * CHUNK), F32),
            pltpu.VMEM((pfb, chan), F32),
            pltpu.VMEM((1, dishes), jnp.int32),
            pltpu.VMEM((2, 2 * chan, 2 * chan), BF16),
            pltpu.VMEM((2, fir, group, chan), F32),
            pltpu.VMEM((band_chans, 2, dishes, beams), F32),
            pltpu.VMEM((band_chans, 2, dishes, beams), BF16),
            pltpu.VMEM((band_chans, 2, dishes, beams), BF16),
            pltpu.VMEM((band_chans, chunks, 2, 2 * CHUNK, beams), F32),
            pltpu.SemaphoreType.DMA((6,)),
            pltpu.SemaphoreType.DMA((2,)),
            pltpu.SemaphoreType.DMA((halves,)),
            pltpu.SemaphoreType.DMA((halves,)),
        ],
        compiler_params=pltpu.CompilerParams(
            collective_id=0, has_side_effects=True, vmem_limit_bytes=60 * 2**20
        ),
    )(
        samples,
        prototype,
        dish_order.reshape(1, dishes),
        jnp.asarray(fourier_matrix(chan)),
        dish_filter,
        beam_weights,
    )
    return jnp.swapaxes(power, 2, 3)


def solution(mesh):
    placed = (P(None, None, ("grp", "band")), P(), P(), P("band", None, None, None, None), P())
    return jax.shard_map(
        functools.partial(body, mesh.shape["band"]),
        mesh=mesh,
        in_specs=placed,
        out_specs=P(("grp", "band"), None, None, None),
        check_vma=False,
    )
```

time: 39.3 us -> 29.5 us (0.75)
  the two profiles are of different devices: /device:TPU:29 before, /device:TPU:0 now
where the time goes in v2:
time: 29.5 us; the launch traced here: 29.4 us
  Pallas kernels  27.9 us (95%)
  local copies, waits for them, and re-layouts  1.47 us (5%)
    pallas_call x1, Pallas kernels, body(): pl.pallas_call(functools.partial(kernel, dims), out_shape=jax.ShapeDtypeS...  27.9 us
    unnamed x1, local copies, waits for them, and re-layouts  1.47 us

profile of v2, /device:TPU:0, one launch (start us, length us, event | category | flops | bytes accessed | tf_op | source)
XLA Modules:
  0.0 29.4 jit_solution(4268261479123079194)
XLA Ops:
  0.0 27.9 %shard_map.64 = f32[1,8,8,192]{3,2,1,0:T(8,128)} custom-call(f32[2,192,256]{2,1,0:T(8,128)} %x_hbm.1, f32[16,128]{1,0:T(8,128)} %proto_hbm.1, s32[1,192]{1,0:T(1,128)} %bitcast.3, bf16[2,256,256]{2,1,0:T(8,128)(2,1)} %constant.2.clone.fourier_hbm, f32[2,8,192,128]{3,2,1,0:T(8,128)} %taps_hbm.1, f32[1,8,2,192,192]{4,3,2,1,0:T(8,128)} %weights_hbm.1), custom_call_target="tpu_custom_call" | custom-call | tf_op jit(solution)/shard_map/pallas_call | solution.py:299
  27.9 1.5 %copy.8 = f32[1,8,192,8]{2,3,1,0:T(8,128)} copy(f32[1,8,192,8]{2,3,1,0:T(8,128)} %bitcast.2) | data formatting | bytes 98304

commit v3 on v2

--- a/solution.py
+++ b/solution.py
@@ -138,34 +138,40 @@
             def _():
                 pltpu.make_async_copy(outgoing, landing, voltage_sems.at[half]).start()
 
-    load_order.wait()
-    row = lax.broadcasted_iota(jnp.int32, (dishes, dishes), 0)
-    dish_of_row = jnp.zeros((dishes, dishes), jnp.int32)
-    for block in range(2 * halves):
-        rest = row - block * rows_half
-        dish = rest // pairs * group + rest % pairs * 2 + block // 2 * SUB + block % 2
-        dish_of_row = jnp.where(rest >= 0, dish, dish_of_row)
-    chosen = jnp.where(order_ref[...] == dish_of_row, 1.0, 0.0).astype(BF16)
-    load_weights.wait()
-
-    @pl.loop(0, band_chans)
-    def _(index):
-        for part in range(2):
-            high, low = split(weights[index, part])
-            beams_high[index, part] = dot(chosen, high).astype(BF16)
-            beams_low[index, part] = dot(chosen, low).astype(BF16)
-
     load_proto.wait()
     load_taps.wait()
     load_fourier.wait()
+
+    step_frames = 16
+
+    def prepare():
+        load_order.wait()
+        row = lax.broadcasted_iota(jnp.int32, (dishes, dishes), 0)
+        dish_of_row = jnp.zeros((dishes, dishes), jnp.int32)
+        for block in range(2 * halves):
+            rest = row - block * rows_half
+            dish = rest // pairs * group + rest % pairs * 2 + block // 2 * SUB + block % 2
+            dish_of_row = jnp.where(rest >= 0, dish, dish_of_row)
+        chosen = jnp.where(order_ref[...] == dish_of_row, 1.0, 0.0).astype(BF16)
+        load_weights.wait()
+
+        @pl.loop(0, band_chans)
+        def _(index):
+            for part in range(2):
+                high, low = split(weights[index, part])
+                beams_high[index, part] = dot(chosen, high).astype(BF16)
+                beams_low[index, part] = dot(chosen, low).astype(BF16)
 
     @pl.when(active)
     def _():
         spectra[:, 0 : fir - 1] = jnp.zeros((2, fir - 1, SUB, chan), F32)
         for half in range(halves):
             voltages[half, 0 : pfb - 1] = jnp.zeros((pfb - 1, 2, SUB, chan), F32)
-        step_frames = 16
-        for half in range(halves):
+
+    for half in range(halves):
+
+        @pl.when(active)
+        def _():
             landed = voltages.at[half, pl.ds(pfb - 1, frames)]
             pltpu.make_async_copy(landed, landed, voltage_sems.at[half]).wait()
 
@@ -233,6 +239,9 @@
                 @pl.when(device == me)
                 def _():
                     pltpu.make_async_copy(source, landing, panel_sems.at[half]).start()
+
+        if half == 0:
+            prepare()
 
     per_chunk = CHUNK // INTEG
     from_frame = lax.broadcasted_iota(jnp.int32, (per_chunk, CHUNK), 1)

time: 29.5 us -> 29.5 us (level)
  no operation moved by 1% of the time
where the time goes in v3:
time: 29.5 us; the launch traced here: 29.4 us
  Pallas kernels  27.9 us (95%)
  local copies, waits for them, and re-layouts  1.47 us (5%)
    pallas_call x1, Pallas kernels, body(): pl.pallas_call(functools.partial(kernel, dims), out_shape=jax.ShapeDtypeS...  27.9 us
    unnamed x1, local copies, waits for them, and re-layouts  1.47 us

profile of v3, /device:TPU:0, one launch (start us, length us, event | category | flops | bytes accessed | tf_op | source)
XLA Modules:
  0.0 29.4 jit_solution(6307216074387954540)
XLA Ops:
  0.0 27.9 %shard_map.64 = f32[1,8,8,192]{3,2,1,0:T(8,128)} custom-call(f32[2,192,256]{2,1,0:T(8,128)} %x_hbm.1, f32[16,128]{1,0:T(8,128)} %proto_hbm.1, s32[1,192]{1,0:T(1,128)} %bitcast.3, bf16[2,256,256]{2,1,0:T(8,128)(2,1)} %constant.2.clone.fourier_hbm, f32[2,8,192,128]{3,2,1,0:T(8,128)} %taps_hbm.1, f32[1,8,2,192,192]{4,3,2,1,0:T(8,128)} %weights_hbm.1), custom_call_target="tpu_custom_call" | custom-call | tf_op jit(solution)/shard_map/pallas_call | solution.py:308
  27.9 1.5 %copy.8 = f32[1,8,192,8]{2,3,1,0:T(8,128)} copy(f32[1,8,192,8]{2,3,1,0:T(8,128)} %bitcast.2) | data formatting | bytes 98304
